TPU v7x, 32 devices: a whole 2x2x4 slice. The times are simulated.
32 devices in a mesh: groups: 2 (over y), seq: 8 (over z, x), heads: 2 (over core).
Axes of the slice: x: 2, y: 2, z: 4, core: 2. Of those that a mesh axis runs over, the one named last changes fastest.
Arguments:
- queries: bfloat16 [8192, 16, 128], P(('groups', 'seq'), 'heads'), parts along dimension 0, may hold values from -128 to 128
- keys: bfloat16 [8192, 16, 128], P(('groups', 'seq'), 'heads'), parts along dimension 0, may hold values from -128 to 128
- values: bfloat16 [8192, 16, 128], P(('groups', 'seq'), 'heads'), parts along dimension 0, may hold values from -6 to 6
Outputs:
- attended: bfloat16 [8192, 16, 128], P(('groups', 'seq'), 'heads'), parts along dimension 0
There are 2 independent parts, one for each index of `groups`. A program takes and returns all parts, laid end to end along the dimension named above; each array names one. Nothing has to cross between parts.
All inputs are finite; a program needn't handle non-finite values.
Results may differ from a plain program's by a relative error of at most 0.0055.
Values may be sent and summed in bfloat16 or wider, within the bound.
A program may use at most 128 MiB of HBM per device.

v0:
```python
import functools
import math

import jax
import jax.numpy as jnp
from jax import lax
from jax.experimental import pallas as pl
from jax.experimental.pallas import tpu as pltpu
from jax.sharding import PartitionSpec as P

BLOCK = 64
QUAD = 4 * BLOCK
HALF = 2 * BLOCK
NEAR = 5 * BLOCK
NEG = -1e30
F32 = jnp.float32
BF16 = jnp.bfloat16


def to_heads(values, scratch, heads):
    count, _, width = values.shape
    scratch[pl.ds(0, count * heads), :] = values.reshape(count * heads, width)
    return [scratch[pl.ds(h, count, stride=heads), :].astype(BF16) for h in range(heads)]


def halved(values):
    count, heads, width = values.shape
    pairs = values.reshape(count // 2, 2, heads, width)
    return pairs[:, 0] + pairs[:, 1]


def across(column, count):
    width = column.shape[1]
    parts = [column] * (count // width)
    if count % width:
        parts.append(column[:, :count % width])
    return jnp.concatenate(parts, 1) if len(parts) > 1 else parts[0]


def with_ones(values):
    return jnp.concatenate([values, jnp.ones_like(values)], 1)


def kernel(size, span, q_ref, k_ref, v_ref, o_ref,
           far, tail0, tailp, sendp, eq, e0, e1, e2, fk,
           bias, acc, top, total, tmp, otmp,
           t_send, t_recv, up_send, up_recv, pr_send, pr_recv):
    rows, heads, width = q_ref.shape
    own = rows // 8
    gain = math.log2(math.e) / math.sqrt(width)
    me = lax.axis_index("seq")
    col = lax.rem(me, 2)
    lev = me // 2
    levels = size // 2
    together = 2 - heads % 2
    pair = me + 1 - 2 * col
    sources = (k_ref, v_ref)

    barrier = pltpu.get_barrier_semaphore()
    for step in (-2, -1, 1, 2):
        @pl.when((me + step >= 0) & (me + step < size))
        def _():
            pl.semaphore_signal(barrier, inc=1, device_id={"seq": me + step},
                                device_id_type=pl.DeviceIdType.MESH)

    def tail_copy(kv, part, target):
        if part == 0:
            src, dst = sources[kv].at[pl.ds(rows - BLOCK, BLOCK)], tail0.at[kv]
        else:
            src, dst = sendp.at[kv], tailp.at[kv]
        return pltpu.make_async_remote_copy(
            src_ref=src, dst_ref=dst, send_sem=t_send.at[kv, part], recv_sem=t_recv.at[kv, part],
            device_id={"seq": target}, device_id_type=pl.DeviceIdType.MESH)

    def up_copy(kv, b, target):
        return pltpu.make_async_remote_copy(
            src_ref=far.at[kv, b], dst_ref=far.at[kv, b],
            send_sem=up_send.at[kv, b], recv_sem=up_recv.at[kv, b],
            device_id={"seq": target}, device_id_type=pl.DeviceIdType.MESH)

    def pair_copy(kv, b):
        return pltpu.make_async_remote_copy(
            src_ref=far.at[kv, b], dst_ref=far.at[kv, b],
            send_sem=pr_send.at[kv, b], recv_sem=pr_recv.at[kv, b],
            device_id={"seq": pair}, device_id_type=pl.DeviceIdType.MESH)

    climbs = lev < levels - 1
    up = jnp.minimum(me + 2, size - 1)
    after = jnp.minimum(me + 1, size - 1)

    def split(kv, c):
        x = sources[kv][pl.ds(c * BLOCK, BLOCK)].astype(F32)
        two = halved(x)
        four = halved(two)
        eight = halved(four)
        two = two * 0.5
        four = four * 0.25
        far[kv, me, pl.ds(c * 8, 8)] = (eight * 0.125).astype(BF16)
        if c >= rows // BLOCK - 4 and c < rows // BLOCK - 1:
            sendp[kv, pl.ds(32 + 16 * (c - rows // BLOCK + 4), 16)] = four.astype(BF16)
        if c == rows // BLOCK - 2:
            sendp[kv, pl.ds(0, 32)] = two.astype(BF16)

    def spread(kv, c):
        x = sources[kv][pl.ds(c * BLOCK, BLOCK)].astype(F32)
        for h, part in enumerate(to_heads(x, tmp, heads)):
            e0[kv, h, pl.ds(BLOCK + c * BLOCK, BLOCK), :] = part
        if c < rows // BLOCK - 2:
            two = halved(x)
            for h, part in enumerate(to_heads(two * 0.5, tmp, heads)):
                e1[kv, h, pl.ds(BLOCK + c * 32, 32), :] = part
            if c < rows // BLOCK - 4:
                four = halved(two)
                for h, part in enumerate(to_heads(four * 0.25, tmp, heads)):
                    e2[kv, h, pl.ds(BLOCK + c * 16, 16), :] = part

    for kv in (1, 0):
        for c in range(rows // BLOCK):
            split(kv, c)

    lower = jnp.minimum(me, 2)
    upper = jnp.minimum(size - 1 - me, 2)
    pl.semaphore_wait(barrier, lower + upper)

    for kv in (1, 0):
        @pl.when(climbs)
        def _():
            up_copy(kv, me, up).start()

        @pl.when(col == 0)
        def _():
            pair_copy(kv, me).start()

    @pl.when(me < size - 1)
    def _():
        for kv in range(2):
            tail_copy(kv, 0, after).start()
            tail_copy(kv, 1, after).start()

    for kv in range(2):
        for c in range(rows // BLOCK):
            spread(kv, c)
    for c in range(rows // BLOCK):
        x = q_ref[pl.ds(c * BLOCK, BLOCK)].astype(F32)
        for h, part in enumerate(to_heads(x, tmp, heads)):
            eq[h, pl.ds(c * BLOCK, BLOCK), :] = part

    i = lax.broadcasted_iota(jnp.int32, (HALF, NEAR), 0)
    j = lax.broadcasted_iota(jnp.int32, (HALF, NEAR), 1)
    is0 = j < 192
    is2 = j >= 256
    level = jnp.where(is0, 0.0, jnp.where(is2, 2.0, 1.0))
    ok01 = jnp.where(is0, jnp.where((j <= i + BLOCK) & ((j >= BLOCK) | (i < BLOCK)), 1, 0),
                     jnp.where((j < 224) | (i >= BLOCK), 1, 0))
    for qd in range(rows // QUAD):
        for hf in range(2):
            ok = jnp.where(is2, jnp.where((j < 288) | (hf == 1), 1, 0), ok01)
            if qd == 0:
                real = (j >= BLOCK) & (j < 192) if hf == 0 else j < 256
                ok = jnp.where(real | (me > 0), ok, 0)
            bias[2 * qd + hf] = jnp.where(ok > 0, level, NEG)

    def near(qd):
        def body(g, _):
            for part in range(2 * together):
                h, hf = g * together + part // 2, part % 2
                at = qd * QUAD + hf * HALF
                q = eq[h, pl.ds(at, HALF), :]
                kk, vv = (jnp.concatenate([
                    e0[kv, h, pl.ds(at, 192), :],
                    e1[kv, h, pl.ds(at // 2, BLOCK), :],
                    e2[kv, h, pl.ds(qd * BLOCK, BLOCK), :]], 0) for kv in range(2))
                s = lax.dot_general(q, kk, (((1,), (1,)), ((), ())), preferred_element_type=F32)
                s = s * gain + bias[2 * qd + hf]
                m = jnp.broadcast_to(jnp.max(s, axis=1, keepdims=True), (HALF, width))
                w = jnp.exp2(s - across(m, NEAR)).astype(BF16)
                both = jnp.dot(w, with_ones(vv), preferred_element_type=F32)
                top[h, pl.ds(at, HALF), :] = m
                acc[h, pl.ds(at, HALF), :] = both[:, :width]
                total[h, pl.ds(at, HALF), :] = both[:, width:]
            return 0
        lax.fori_loop(0, heads // together, body, 0)

    for qd in range(1, rows // QUAD):
        near(qd)

    def pass_on(r, _):
        b = me - 2 * r
        for kv in range(2):
            up_copy(kv, b, up).wait_recv()

            @pl.when(climbs)
            def _():
                up_copy(kv, b, up).start()

            if kv == 0:
                pair_copy(kv, b).start()
            else:
                @pl.when(col == 1)
                def _():
                    pair_copy(kv, b).start()

        @pl.when((col == 1) & climbs)
        def _():
            even_on(r)
        return 0

    def even_on(r):
        b = me + 1 - 2 * r

        @pl.when(r == 1)
        def _():
            pair_copy(1, b).wait_recv()

        @pl.when(r > 1)
        def _():
            up_copy(1, b, up).wait_recv()

        up_copy(1, b, up).start()

    lax.fori_loop(1, lev + 1, pass_on, 0)

    @pl.when((col == 1) & climbs)
    def _():
        even_on(lev + 1)

    @pl.when(me == 0)
    def _():
        for kv in range(2):
            for h in range(heads):
                e0[kv, h, pl.ds(0, BLOCK), :] = jnp.zeros((BLOCK, width), BF16)
                e1[kv, h, pl.ds(0, BLOCK), :] = jnp.zeros((BLOCK, width), BF16)
                e2[kv, h, pl.ds(0, BLOCK), :] = jnp.zeros((BLOCK, width), BF16)

    @pl.when(me > 0)
    def _():
        for kv in range(2):
            tail_copy(kv, 0, after).wait_recv()
            tail_copy(kv, 1, after).wait_recv()
            x = tail0[kv].astype(F32)
            for h, part in enumerate(to_heads(x, tmp, heads)):
                e0[kv, h, pl.ds(0, BLOCK), :] = part
            two = halved(x)
            four = halved(two)
            for h, part in enumerate(to_heads(two * 0.5, tmp, heads)):
                e1[kv, h, pl.ds(32, 32), :] = part
            for h, part in enumerate(to_heads(four * 0.25, tmp, heads)):
                e2[kv, h, pl.ds(48, 16), :] = part
            y = tailp[kv].astype(F32)
            for h, part in enumerate(to_heads(y, tmp, heads)):
                e1[kv, h, pl.ds(0, 32), :] = part[:32]
                e2[kv, h, pl.ds(0, 48), :] = part[32:]

    near(0)

    def arrange(s, _):
        b = me - 1 - s
        place = pl.multiple_of(s * own, own)
        even = lax.rem(s, 2) == 0

        @pl.when((s < me) & even)
        def _():
            pair_copy(0, b).wait_recv()

            @pl.when(col == 0)
            def _():
                pair_copy(1, b).wait_recv()

            @pl.when((col == 1) & jnp.logical_not(climbs) & (s == 0))
            def _():
                pair_copy(1, b).wait_recv()

            @pl.when((col == 1) & jnp.logical_not(climbs) & (s > 0))
            def _():
                up_copy(1, b, up).wait_recv()

        @pl.when(s < me)
        def _():
            for kv in range(2):
                x = far[kv, b].astype(F32)
                for h, part in enumerate(to_heads(x, tmp, heads)):
                    fk[kv, h, pl.ds(place, own), :] = part

        @pl.when(s >= me)
        def _():
            for kv in range(2):
                for h in range(heads):
                    fk[kv, h, pl.ds(place, own), :] = jnp.zeros((own, width), BF16)
        return 0

    wide = span * own

    def chunk(c, _):
        lax.fori_loop(c * span, (c + 1) * span, arrange, 0)
        start = pl.multiple_of(c * wide, wide)
        place = start + lax.broadcasted_iota(jnp.int32, (1, wide), 1)
        known = jnp.where(place < own * me, 3.0, NEG)
        masks = [jnp.where((place >= own // 2) & (place < own), NEG, known), known]

        def body(h, _):
            for qd in range(rows // QUAD):
                for hf in range(2):
                    at = qd * QUAD + hf * HALF
                    m = top[h, pl.ds(at, HALF), :]
                    s = lax.dot_general(eq[h, pl.ds(at, HALF), :], fk[0, h, pl.ds(start, wide), :],
                                        (((1,), (1,)), ((), ())), preferred_element_type=F32)
                    s = s * gain + masks[min(qd, 1)]
                    fresh = jnp.maximum(m, jnp.max(s, axis=1, keepdims=True))
                    fade = jnp.exp2(m - fresh)
                    w = jnp.exp2(s - across(fresh, wide)).astype(BF16)
                    both = jnp.dot(w, with_ones(fk[1, h, pl.ds(start, wide), :]),
                                   preferred_element_type=F32)
                    top[h, pl.ds(at, HALF), :] = fresh
                    acc[h, pl.ds(at, HALF), :] = acc[h, pl.ds(at, HALF), :] * fade + both[:, :width]
                    total[h, pl.ds(at, HALF), :] = (
                        total[h, pl.ds(at, HALF), :] * fade + both[:, width:])
            return 0

        lax.fori_loop(0, heads, body, 0)
        return 0

    lax.fori_loop(0, (me + span - 1) // span, chunk, 0)
    for c in range(rows // HALF):
        for h in range(heads):
            otmp[pl.ds(h, HALF, stride=heads), :] = (
                acc[h, pl.ds(c * HALF, HALF), :] / total[h, pl.ds(c * HALF, HALF), :])
        o_ref[pl.ds(c * HALF, HALF)] = otmp[...].reshape(HALF, heads, width).astype(BF16)

    @pl.when(me < size - 1)
    def _():
        for kv in range(2):
            tail_copy(kv, 0, after).wait_send()
            tail_copy(kv, 1, after).wait_send()

    @pl.when(col == 0)
    def _():
        for kv in range(2):
            pair_copy(kv, me).wait_send()

    def sent(r, _):
        b = me - 2 * r

        @pl.when(climbs)
        def _():
            for kv in range(2):
                up_copy(kv, b, up).wait_send()

            @pl.when(col == 1)
            def _():
                up_copy(1, b - 1, up).wait_send()

        @pl.when(r > 0)
        def _():
            pair_copy(0, b).wait_send()

            @pl.when(col == 1)
            def _():
                pair_copy(1, b).wait_send()
        return 0

    lax.fori_loop(0, lev + 1, sent, 0)


def shards(size, queries, keys, values):
    rows, heads, width = queries.shape
    own = rows // 8
    span = max(n for n in range(1, min(size, 4) + 1) if size % n == 0)
    vmem = pl.BlockSpec(memory_space=pltpu.VMEM)
    return pl.pallas_call(
        functools.partial(kernel, size, span),
        out_shape=jax.ShapeDtypeStruct((rows, heads, width), BF16),
        in_specs=[vmem] * 3,
        out_specs=vmem,
        scratch_shapes=[
            pltpu.VMEM((2, size, own, heads, width), BF16),
            pltpu.VMEM((2, BLOCK, heads, width), BF16),
            pltpu.VMEM((2, 80, heads, width), BF16),
            pltpu.VMEM((2, 80, heads, width), BF16),
            pltpu.VMEM((heads, rows, width), BF16),
            pltpu.VMEM((2, heads, rows + BLOCK, width), BF16),
            pltpu.VMEM((2, heads, rows // 2, width), BF16),
            pltpu.VMEM((2, heads, rows // 4, width), BF16),
            pltpu.VMEM((2, heads, size * own, width), BF16),
            pltpu.VMEM((rows // HALF, HALF, NEAR), F32),
            pltpu.VMEM((heads, rows, width), F32),
            pltpu.VMEM((heads, rows, width), F32),
            pltpu.VMEM((heads, rows, width), F32),
            pltpu.VMEM((80 * heads, width), F32),
            pltpu.VMEM((HALF * heads, width), F32),
            pltpu.SemaphoreType.DMA((2, 2)),
            pltpu.SemaphoreType.DMA((2, 2)),
            pltpu.SemaphoreType.DMA((2, size)),
            pltpu.SemaphoreType.DMA((2, size)),
            pltpu.SemaphoreType.DMA((2, size)),
            pltpu.SemaphoreType.DMA((2, size)),
        ],
        compiler_params=pltpu.CompilerParams(
            collective_id=0, has_side_effects=True, vmem_limit_bytes=60 * 2**20),
    )(queries, keys, values)


def solution(mesh):
    spec = P(("groups", "seq"), "heads", None)
    return jax.shard_map(
        functools.partial(shards, mesh.shape["seq"]),
        mesh=mesh, in_specs=(spec,) * 3, out_specs=spec, check_vma=False)
```

profile of v0, /device:TPU:30, one launch (start us, length us, event | category | flops | bytes accessed | tf_op | source)
XLA Modules:
  0.0 55.1 jit_solution(4053679698139137119)
XLA Ops:
  0.0 52.9 %shard_map.37 = bf16[512,8,128]{2,1,0:T(8,128)(2,1)} custom-call(bf16[512,8,128]{2,1,0:T(8,128)(2,1)} %q_ref.1, bf16[512,8,128]{2,1,0:T(8,128)(2,1)} %k_ref.1, bf16[512,8,128]{2,1,0:T(8,128)(2,1)} %v_ref.1), custom_call_target="tpu_custom_call" | custom-call | tf_op jit(solution)/shard_map/pallas_call | solution.py:369
  52.9 2.3 %copy.5 = bf16[512,8,128]{2,1,0:T(8,128)(2,1)} copy(bf16[512,8,128]{2,1,0:T(8,128)(2,1)} %shard_map.37) | data formatting | bytes 2097152
where the time goes:
time: 55.3 us; the launch traced here: 55.1 us
  Pallas kernels  52.9 us (96%)
  local copies, waits for them, and re-layouts  2.26 us (4%)
    pallas_call x1, Pallas kernels, shards(): pl.pallas_call(functools.partial(kernel, size, span), out_shape=jax.Shape...  52.9 us
    unnamed x1, local copies, waits for them, and re-layouts  2.26 us

commit v1 on v0

v1 whole, which is shorter than its diff:
```python
import functools
import math

import jax
import jax.numpy as jnp
from jax import lax
from jax.experimental import pallas as pl
from jax.experimental.pallas import tpu as pltpu
from jax.sharding import PartitionSpec as P

BLOCK = 64
QUAD = 4 * BLOCK
HALF = 2 * BLOCK
NEAR = 6 * BLOCK
NEG = -1e30
F32 = jnp.float32
BF16 = jnp.bfloat16


def to_heads(values, scratch, heads):
    count, _, width = values.shape
    scratch[pl.ds(0, count * heads), :] = values.reshape(count * heads, width)
    return [scratch[pl.ds(h, count, stride=heads), :].astype(BF16) for h in range(heads)]


def halved(values):
    count, heads, width = values.shape
    pairs = values.reshape(count // 2, 2, heads, width)
    return pairs[:, 0] + pairs[:, 1]


def across(column, count):
    width = column.shape[1]
    return jnp.concatenate([column] * (count // width), 1) if count > width else column


def with_ones(values):
    return jnp.concatenate([values, jnp.ones_like(values)], 1)


def kernel(size, q_ref, k_ref, v_ref, o_ref,
           far, tail, thru, sendp, eq, e0, e1, e2, ex, fk,
           bias, acc, top, total, tmp, otmp,
           recv, up_send, side_send, t_send, t_recv, r_send, r_recv):
    rows, heads, width = q_ref.shape
    own = rows // 8
    blocks = rows // BLOCK
    gain = math.log2(math.e) / math.sqrt(width)
    me = lax.axis_index("seq")
    col = lax.rem(me, 2)
    lev = me // 2
    levels = size // 2
    together = 2 - heads % 2
    climbs = lev < levels - 1
    pair = me + 1 - 2 * col
    up = jnp.minimum(me + 2, size - 1)
    sources = (k_ref, v_ref)

    def remote(src, dst, send, got, target):
        return pltpu.make_async_remote_copy(
            src_ref=src, dst_ref=dst, send_sem=send, recv_sem=got,
            device_id={"seq": target}, device_id_type=pl.DeviceIdType.MESH)

    def up_copy(kv, b):
        return remote(far.at[kv, b], far.at[kv, b], up_send.at[kv, b], recv.at[kv, b], up)

    def side_copy(kv, b):
        return remote(far.at[kv, b], far.at[kv, b], side_send.at[kv, b], recv.at[kv, b], pair)

    def tail_source(kv, part):
        return sources[kv].at[pl.ds(rows - BLOCK, BLOCK)] if part == 0 else sendp.at[kv]

    def tail_copy(kv, part):
        return remote(tail_source(kv, part), tail.at[kv, part], t_send.at[kv, part], t_recv.at[kv, part], pair)

    def thru_copy(kv, part):
        return remote(tail_source(kv, part), thru.at[kv, part], t_send.at[kv, part], r_recv.at[kv, part], pair)

    def relay_copy(kv, part):
        return remote(thru.at[kv, part], tail.at[kv, part], r_send.at[kv, part], t_recv.at[kv, part], up)

    barrier = pltpu.get_barrier_semaphore()
    for step in (-2, 2):
        @pl.when((me + step >= 0) & (me + step < size))
        def _():
            pl.semaphore_signal(barrier, inc=1, device_id={"seq": me + step},
                                device_id_type=pl.DeviceIdType.MESH)
    pl.semaphore_signal(barrier, inc=1, device_id={"seq": pair}, device_id_type=pl.DeviceIdType.MESH)

    def split(kv, c):
        x = sources[kv][pl.ds(c * BLOCK, BLOCK)].astype(F32)
        two = halved(x)
        four = halved(two)
        eight = halved(four)
        far[kv, me, pl.ds(c * 8, 8)] = (eight * 0.125).astype(BF16)
        if c == blocks - 2:
            sendp[kv, pl.ds(0, 32)] = (two * 0.5).astype(BF16)
        if blocks - 4 <= c < blocks - 2:
            sendp[kv, pl.ds(32 + 16 * (c - blocks + 4), 16)] = (four * 0.25).astype(BF16)

    def spread(kv, c):
        x = sources[kv][pl.ds(c * BLOCK, BLOCK)].astype(F32)
        for h, part in enumerate(to_heads(x, tmp, heads)):
            e0[kv, h, pl.ds(BLOCK + c * BLOCK, BLOCK), :] = part
        if c < blocks - 2:
            two = halved(x)
            for h, part in enumerate(to_heads(two * 0.5, tmp, heads)):
                e1[kv, h, pl.ds(BLOCK + c * 32, 32), :] = part
            if c < blocks - 4:
                four = halved(two)
                for h, part in enumerate(to_heads(four * 0.25, tmp, heads)):
                    e2[kv, h, pl.ds(BLOCK + c * 16, 16), :] = part

    for kv in (1, 0):
        for c in range(blocks):
            split(kv, c)

    pl.semaphore_wait(barrier, 1 + jnp.where(lev > 0, 1, 0) + jnp.where(climbs, 1, 0))

    @pl.when(col == 0)
    def _():
        side_copy(1, me).start()
        side_copy(0, me).start()

        @pl.when(climbs)
        def _():
            up_copy(0, me).start()
        for kv in range(2):
            for part in range(2):
                tail_copy(kv, part).start()

    @pl.when((col == 1) & climbs)
    def _():
        up_copy(0, me).start()
        up_copy(1, me).start()
        for kv in range(2):
            for part in range(2):
                thru_copy(kv, part).start()

    for kv in range(2):
        for c in range(blocks):
            spread(kv, c)
    for c in range(blocks):
        x = q_ref[pl.ds(c * BLOCK, BLOCK)].astype(F32)
        for h, part in enumerate(to_heads(x, tmp, heads)):
            eq[h, pl.ds(c * BLOCK, BLOCK), :] = part

    i = lax.broadcasted_iota(jnp.int32, (HALF, NEAR), 0)
    j = lax.broadcasted_iota(jnp.int32, (HALF, NEAR), 1)
    is0 = j < 192
    is2 = j >= 256
    is3 = j >= 320
    level = jnp.where(is0, 0.0, jnp.where(is3, 3.0, jnp.where(is2, 2.0, 1.0)))
    ok01 = jnp.where(is0, jnp.where((j <= i + BLOCK) & ((j >= BLOCK) | (i < BLOCK)), 1, 0),
                     jnp.where((j < 224) | (i >= BLOCK), 1, 0))
    for qd in range(rows // QUAD):
        ok3 = jnp.where((col == 1) & ((j < 320 + own // 2) | (qd > 0)), 1, 0)
        for hf in range(2):
            ok = jnp.where(is2, jnp.where((j < 288) | (hf == 1), 1, 0), ok01)
            if qd == 0:
                real = (j >= BLOCK) & (j < 192) if hf == 0 else j < 256
                ok = jnp.where(real | (me > 0), ok, 0)
            ok = jnp.where(is3, ok3, ok)
            bias[2 * qd + hf] = jnp.where(ok > 0, level, NEG)

    def near(qd, first, count):
        def body(g, _):
            for part in range(2 * together):
                h, hf = g * together + part // 2, part % 2
                at = qd * QUAD + hf * HALF
                q = eq[h, pl.ds(at, HALF), :]
                kk, vv = (jnp.concatenate([
                    e0[kv, h, pl.ds(at, 192), :],
                    e1[kv, h, pl.ds(at // 2, BLOCK), :],
                    e2[kv, h, pl.ds(qd * BLOCK, BLOCK), :],
                    ex[kv, h]], 0) for kv in range(2))
                s = lax.dot_general(q, kk, (((1,), (1,)), ((), ())), preferred_element_type=F32)
                s = s * gain + bias[2 * qd + hf]
                m = jnp.broadcast_to(jnp.max(s, axis=1, keepdims=True), (HALF, width))
                w = jnp.exp2(s - across(m, NEAR)).astype(BF16)
                both = jnp.dot(w, with_ones(vv), preferred_element_type=F32)
                top[h, pl.ds(at, HALF), :] = m
                acc[h, pl.ds(at, HALF), :] = both[:, :width]
                total[h, pl.ds(at, HALF), :] = both[:, width:]
            return 0
        lax.fori_loop(first, first + count, body, 0)

    def extra():
        @pl.when(col == 1)
        def _():
            side_copy(0, me - 1).wait_recv()
            for kv in range(2):
                for h, part in enumerate(to_heads(far[kv, me - 1].astype(F32), tmp, heads)):
                    ex[kv, h] = part

        @pl.when(col == 0)
        def _():
            ex[...] = jnp.zeros_like(ex)

    def previous():
        @pl.when(me == 0)
        def _():
            for kv in range(2):
                for h in range(heads):
                    for e in (e0, e1, e2):
                        e[kv, h, pl.ds(0, BLOCK), :] = jnp.zeros((BLOCK, width), BF16)

        @pl.when(me > 0)
        def _():
            for kv in range(2):
                for part in range(2):
                    tail_copy(kv, part).wait_recv()
                x = tail[kv, 0].astype(F32)
                two = halved(x)
                four = halved(two)
                y = tail[kv, 1].astype(F32)
                late = halved(y[:32])
                for h, part in enumerate(to_heads(x, tmp, heads)):
                    e0[kv, h, pl.ds(0, BLOCK), :] = part
                for h, part in enumerate(to_heads(two * 0.5, tmp, heads)):
                    e1[kv, h, pl.ds(32, 32), :] = part
                for h, part in enumerate(to_heads(four * 0.25, tmp, heads)):
                    e2[kv, h, pl.ds(48, 16), :] = part
                for h, part in enumerate(to_heads(late * 0.5, tmp, heads)):
                    e2[kv, h, pl.ds(32, 16), :] = part
                for h, part in enumerate(to_heads(y, tmp, heads)):
                    e1[kv, h, pl.ds(0, 32), :] = part[:32]
                    e2[kv, h, pl.ds(0, 32), :] = part[32:]

    def distant(r):
        odd = me - 2 * r + 1 - col
        even = me - 2 * r - col

        @pl.when(col == 1)
        def _():
            side_copy(0, even).wait_recv()

        @pl.when(col == 0)
        def _():
            side_copy(0, odd).wait_recv()
            side_copy(1, odd).wait_recv()
        for kv in range(2):
            for n, b in enumerate((odd, even)):
                for h, part in enumerate(to_heads(far[kv, b].astype(F32), tmp, heads)):
                    fk[kv, h, pl.ds(n * own, own), :] = part
        place = lax.broadcasted_iota(jnp.int32, (1, 2 * own), 1)
        hide = jnp.where((col == 0) & (r == 1) & (place >= own // 2) & (place < own), NEG, 0.0)

        def body(h, _):
            for qd in range(rows // QUAD):
                for hf in range(2):
                    at = qd * QUAD + hf * HALF
                    m = top[h, pl.ds(at, HALF), :]
                    s = lax.dot_general(eq[h, pl.ds(at, HALF), :], fk[0, h],
                                        (((1,), (1,)), ((), ())), preferred_element_type=F32)
                    if qd == 0:
                        s = s + hide
                    peak = jnp.max(s, axis=1, keepdims=True) * gain + 3.0
                    fresh = jnp.maximum(m, peak)
                    fade = jnp.exp2(m - fresh)
                    w = jnp.exp2(s * gain - across(fresh - 3.0, 2 * own)).astype(BF16)
                    both = jnp.dot(w, with_ones(fk[1, h]), preferred_element_type=F32)
                    top[h, pl.ds(at, HALF), :] = fresh
                    acc[h, pl.ds(at, HALF), :] = acc[h, pl.ds(at, HALF), :] * fade + both[:, :width]
                    total[h, pl.ds(at, HALF), :] = (
                        total[h, pl.ds(at, HALF), :] * fade + both[:, width:])
            return 0

        lax.fori_loop(0, heads, body, 0)

    groups = heads // together
    early = (groups + 1) // 2

    def turn(n, _):
        r = (n - 1) // 3 + 1
        part = lax.rem(n - 1, 3)

        @pl.when((col == 1) & (n == 1))
        def _():
            side_copy(1, me - 1).wait_recv()

            @pl.when(climbs)
            def _():
                up_copy(1, me - 1).start()

        @pl.when((col == 1) & (r <= lev))
        def _():
            kv = jnp.minimum(part, 1)
            b = me - 2 * r - jnp.where(part == 2, 1, 0)
            up_copy(kv, b).wait_recv()

            @pl.when(climbs)
            def _():
                up_copy(kv, b).start()

            @pl.when((part < 2) | (r == 1))
            def _():
                side_copy(kv, b).start()

        @pl.when((col == 0) & (n <= lev))
        def _():
            b = me - 2 * n
            up_copy(0, b).wait_recv()
            side_copy(0, b).start()

            @pl.when(climbs)
            def _():
                up_copy(0, b).start()

        @pl.when((col == 0) & climbs & (n <= 4))
        def _():
            kv, part = (n - 1) // 2, lax.rem(n - 1, 2)
            remote(thru.at[kv, part], thru.at[kv, part], r_send.at[kv, part], r_recv.at[kv, part], pair).wait_recv()
            relay_copy(kv, part).start()

        @pl.when((col == 0) & (n > 4) & (n - 4 <= lev))
        def _():
            b = me - 2 * (n - 4)
            up_copy(1, b).wait_recv()

            @pl.when(climbs)
            def _():
                up_copy(1, b).start()

        @pl.when(n == 2)
        def _():
            extra()

        @pl.when((n == 2) | (n == 3))
        def _():
            for qd in range(1, rows // QUAD):
                near(qd, (n - 2) * early, jnp.where(n == 2, early, groups - early))

        @pl.when(n == 6)
        def _():
            previous()
            near(0, 0, groups)

        gone = jnp.where(n <= 9, n - 6, n // 3)

        @pl.when((gone >= 1) & (gone <= lev) & ((n <= 9) | (lax.rem(n, 3) == 0)))
        def _():
            distant(gone)
        return 0

    lax.fori_loop(1, jnp.maximum(6 + lev, 3 * lev) + 1, turn, 0)

    for c in range(rows // HALF):
        for h in range(heads):
            otmp[pl.ds(h, HALF, stride=heads), :] = (
                acc[h, pl.ds(c * HALF, HALF), :] / total[h, pl.ds(c * HALF, HALF), :])
        o_ref[pl.ds(c * HALF, HALF)] = otmp[...].reshape(HALF, heads, width).astype(BF16)

    @pl.when(col == 0)
    def _():
        side_copy(1, me).wait_send()
        side_copy(0, me).wait_send()
        for kv in range(2):
            for part in range(2):
                tail_copy(kv, part).wait_send()

        @pl.when(climbs)
        def _():
            up_copy(0, me).wait_send()
            for kv in range(2):
                for part in range(2):
                    relay_copy(kv, part).wait_send()

    @pl.when((col == 1) & climbs)
    def _():
        up_copy(0, me).wait_send()
        up_copy(1, me).wait_send()
        up_copy(1, me - 1).wait_send()
        for kv in range(2):
            for part in range(2):
                thru_copy(kv, part).wait_send()

    def sent(r, _):
        b = me - 2 * r
        side_copy(0, b).wait_send()

        @pl.when(climbs)
        def _():
            up_copy(0, b).wait_send()
            up_copy(1, b).wait_send()

        @pl.when(col == 1)
        def _():
            side_copy(1, b).wait_send()

            @pl.when(climbs)
            def _():
                up_copy(1, b - 1).wait_send()

            @pl.when(r == 1)
            def _():
                side_copy(1, b - 1).wait_send()
        return 0

    lax.fori_loop(1, lev + 1, sent, 0)


def shards(size, queries, keys, values):
    rows, heads, width = queries.shape
    own = rows // 8
    vmem = pl.BlockSpec(memory_space=pltpu.VMEM)
    return pl.pallas_call(
        functools.partial(kernel, size),
        out_shape=jax.ShapeDtypeStruct((rows, heads, width), BF16),
        in_specs=[vmem] * 3,
        out_specs=vmem,
        scratch_shapes=[
            pltpu.VMEM((2, size, own, heads, width), BF16),
            pltpu.VMEM((2, 2, BLOCK, heads, width), BF16),
            pltpu.VMEM((2, 2, BLOCK, heads, width), BF16),
            pltpu.VMEM((2, BLOCK, heads, width), BF16),
            pltpu.VMEM((heads, rows, width), BF16),
            pltpu.VMEM((2, heads, rows + BLOCK, width), BF16),
            pltpu.VMEM((2, heads, rows // 2, width), BF16),
            pltpu.VMEM((2, heads, rows // 4, width), BF16),
            pltpu.VMEM((2, heads, own, width), BF16),
            pltpu.VMEM((2, heads, 2 * own, width), BF16),
            pltpu.VMEM((rows // HALF, HALF, NEAR), F32),
            pltpu.VMEM((heads, rows, width), F32),
            pltpu.VMEM((heads, rows, width), F32),
            pltpu.VMEM((heads, rows, width), F32),
            pltpu.VMEM((80 * heads, width), F32),
            pltpu.VMEM((HALF * heads, width), F32),
            pltpu.SemaphoreType.DMA((2, size)),
            pltpu.SemaphoreType.DMA((2, size)),
            pltpu.SemaphoreType.DMA((2, size)),
            pltpu.SemaphoreType.DMA((2, 2)),
            pltpu.SemaphoreType.DMA((2, 2)),
            pltpu.SemaphoreType.DMA((2, 2)),
            pltpu.SemaphoreType.DMA((2, 2)),
        ],
        compiler_params=pltpu.CompilerParams(
            collective_id=0, has_side_effects=True, vmem_limit_bytes=60 * 2**20),
    )(queries, keys, values)


def solution(mesh):
    spec = P(("groups", "seq"), "heads", None)
    return jax.shard_map(
        functools.partial(shards, mesh.shape["seq"]),
        mesh=mesh, in_specs=(spec,) * 3, out_specs=spec, check_vma=False)
```

time: 55.3 us -> 66.3 us (1.20)
  the two profiles are of different devices: /device:TPU:30 before, /device:TPU:28 now
where the time goes in v1:
time: 66.3 us; the launch traced here: 66.1 us
  Pallas kernels  63.8 us (96%)
  local copies, waits for them, and re-layouts  2.26 us (3%)
    pallas_call x1, Pallas kernels, shards(): pl.pallas_call(functools.partial(kernel, size), out_shape=jax.ShapeDtypeS...  63.8 us
    unnamed x1, local copies, waits for them, and re-layouts  2.26 us

profile of v1, /device:TPU:28, one launch (start us, length us, event | category | flops | bytes accessed | tf_op | source)
XLA Modules:
  0.0 66.1 jit_solution(15557362887656840924)
XLA Ops:
  0.0 63.8 %shard_map.37 = bf16[512,8,128]{2,1,0:T(8,128)(2,1)} custom-call(bf16[512,8,128]{2,1,0:T(8,128)(2,1)} %q_ref.1, bf16[512,8,128]{2,1,0:T(8,128)(2,1)} %k_ref.1, bf16[512,8,128]{2,1,0:T(8,128)(2,1)} %v_ref.1), custom_call_target="tpu_custom_call" | custom-call | tf_op jit(solution)/shard_map/pallas_call | solution.py:407
  63.9 2.3 %copy.5 = bf16[512,8,128]{2,1,0:T(8,128)(2,1)} copy(bf16[512,8,128]{2,1,0:T(8,128)(2,1)} %shard_map.37) | data formatting | bytes 2097152

commit v2 on v1

v2 whole, which is shorter than its diff:
```python
import functools
import math

import jax
import jax.numpy as jnp
from jax import lax
from jax.experimental import pallas as pl
from jax.experimental.pallas import tpu as pltpu
from jax.sharding import PartitionSpec as P

BLOCK = 64
QUAD = 4 * BLOCK
HALF = 2 * BLOCK
NEAR = 6 * BLOCK
NEG = -1e30
F32 = jnp.float32
BF16 = jnp.bfloat16


def to_heads(values, scratch, heads):
    count, _, width = values.shape
    scratch[pl.ds(0, count * heads), :] = values.reshape(count * heads, width)
    return [scratch[pl.ds(h, count, stride=heads), :].astype(BF16) for h in range(heads)]


def halved(values):
    count, heads, width = values.shape
    pairs = values.reshape(count // 2, 2, heads, width)
    return pairs[:, 0] + pairs[:, 1]


def across(column, count):
    width = column.shape[1]
    return jnp.concatenate([column] * (count // width), 1) if count > width else column


def with_ones(values):
    return jnp.concatenate([values, jnp.ones_like(values)], 1)


def kernel(size, q_ref, k_ref, v_ref, o_ref,
           far, tail, thru, sendp, eq, e0, e1, e2, before, fk,
           mask1, mask0, maskt, acc, top, total, tmp, otmp,
           recv, up_send, side_send, t_send, t_recv, r_send, r_recv):
    rows, heads, width = q_ref.shape
    own = rows // 8
    blocks = rows // BLOCK
    gain = math.log2(math.e) / math.sqrt(width)
    me = lax.axis_index("seq")
    col = lax.rem(me, 2)
    lev = me // 2
    levels = size // 2
    together = 2 - heads % 2
    groups = heads // together
    early = (groups + 1) // 2
    climbs = lev < levels - 1
    pair = me + 1 - 2 * col
    up = jnp.minimum(me + 2, size - 1)
    sources = (k_ref, v_ref)

    def remote(src, dst, send, got, target):
        return pltpu.make_async_remote_copy(
            src_ref=src, dst_ref=dst, send_sem=send, recv_sem=got,
            device_id={"seq": target}, device_id_type=pl.DeviceIdType.MESH)

    def up_copy(kv, b):
        return remote(far.at[kv, b], far.at[kv, b], up_send.at[kv, b], recv.at[kv, b], up)

    def side_copy(kv, b):
        return remote(far.at[kv, b], far.at[kv, b], side_send.at[kv, b], recv.at[kv, b], pair)

    def tail_source(kv, part):
        return sources[kv].at[pl.ds(rows - BLOCK, BLOCK)] if part == 0 else sendp.at[kv]

    def tail_copy(kv, part):
        return remote(tail_source(kv, part), tail.at[kv, part], t_send.at[kv, part], t_recv.at[kv, part], pair)

    def thru_copy(kv, part):
        return remote(tail_source(kv, part), thru.at[kv, part], t_send.at[kv, part], r_recv.at[kv, part], pair)

    def relay_copy(kv, part):
        return remote(thru.at[kv, part], tail.at[kv, part], r_send.at[kv, part], t_recv.at[kv, part], up)

    barrier = pltpu.get_barrier_semaphore()
    for step in (-2, 2):
        @pl.when((me + step >= 0) & (me + step < size))
        def _():
            pl.semaphore_signal(barrier, inc=1, device_id={"seq": me + step},
                                device_id_type=pl.DeviceIdType.MESH)
    pl.semaphore_signal(barrier, inc=1, device_id={"seq": pair}, device_id_type=pl.DeviceIdType.MESH)

    def split(kv, c):
        x = sources[kv][pl.ds(c * BLOCK, BLOCK)].astype(F32)
        two = halved(x)
        four = halved(two)
        eight = halved(four)
        far[kv, me, pl.ds(c * 8, 8)] = (eight * 0.125).astype(BF16)
        if c == blocks - 2:
            sendp[kv, pl.ds(0, 32)] = (two * 0.5).astype(BF16)
        if blocks - 4 <= c < blocks - 2:
            sendp[kv, pl.ds(32 + 16 * (c - blocks + 4), 16)] = (four * 0.25).astype(BF16)

    def spread(kv, c):
        x = sources[kv][pl.ds(c * BLOCK, BLOCK)].astype(F32)
        for h, part in enumerate(to_heads(x, tmp, heads)):
            e0[kv, h, pl.ds(c * BLOCK, BLOCK), :] = part
        if c < blocks - 2:
            two = halved(x)
            for h, part in enumerate(to_heads(two * 0.5, tmp, heads)):
                e1[kv, h, pl.ds(c * 32, 32), :] = part
            if c < blocks - 4:
                four = halved(two)
                for h, part in enumerate(to_heads(four * 0.25, tmp, heads)):
                    e2[kv, h, pl.ds(c * 16, 16), :] = part

    for kv in (1, 0):
        for c in range(blocks):
            split(kv, c)

    pl.semaphore_wait(barrier, 1 + jnp.where(lev > 0, 1, 0) + jnp.where(climbs, 1, 0))

    @pl.when(col == 0)
    def _():
        side_copy(1, me).start()
        side_copy(0, me).start()

        @pl.when(climbs)
        def _():
            up_copy(0, me).start()

        @pl.when(lev < levels - 2)
        def _():
            up_copy(1, me).start()

    @pl.when((col == 1) & climbs)
    def _():
        up_copy(0, me).start()
        up_copy(1, me).start()
        for kv in range(2):
            for part in range(2):
                thru_copy(kv, part).start()

    for kv in range(2):
        for c in range(blocks):
            spread(kv, c)
    for c in range(blocks):
        x = q_ref[pl.ds(c * BLOCK, BLOCK)].astype(F32)
        for h, part in enumerate(to_heads(x, tmp, heads)):
            eq[h, pl.ds(c * BLOCK, BLOCK), :] = part

    def grid(count):
        return (lax.broadcasted_iota(jnp.int32, (HALF, count), 0),
                lax.broadcasted_iota(jnp.int32, (HALF, count), 1))

    i, j = grid(NEAR)
    level = jnp.where(j < 192, 0.0, jnp.where(j < 256, 1.0, jnp.where(j < 320, 2.0, 3.0)))
    seen01 = jnp.where(j < 192, jnp.where((j <= i + BLOCK) & ((j >= BLOCK) | (i < BLOCK)), 1, 0),
                       jnp.where((j < 224) | (i >= BLOCK), 1, 0))
    for hf in range(2):
        seen = jnp.where(j < 256, seen01, jnp.where(j < 320, jnp.where((j < 288) | (hf == 1), 1, 0), col))
        mask1[hf] = jnp.where(seen > 0, level, NEG)
    i, j = grid(HALF)
    mask0[:, pl.ds(0, HALF)] = jnp.where(j <= i, 0.0, NEG)
    i, j = grid(2 * HALF)
    seen0 = jnp.where(j < 192, jnp.where((j <= i + BLOCK) & ((j >= BLOCK) | (i < BLOCK)), 1, 0),
                      jnp.where((j < 224) | (i >= BLOCK), 1, 0))
    mask0[:, pl.ds(HALF, 2 * HALF)] = jnp.where(seen0 > 0, jnp.where(j < 192, 0.0, 1.0), NEG)
    last = jnp.where(j < 192 + own // 2, col, 0)
    seent = jnp.where(j < 64, jnp.where(i < BLOCK, 1, 0),
                      jnp.where(j < 128, jnp.where((j < 96) | (i >= BLOCK), 1, 0),
                                jnp.where(j < 192, jnp.where(j < 160, 1, 0), last)))
    level = jnp.where(j < 64, 0.0, jnp.where(j < 128, 1.0, jnp.where(j < 192, 2.0, 3.0)))
    maskt[:, pl.ds(0, 2 * HALF)] = jnp.where(seent > 0, level, NEG)
    i, j = grid(HALF)
    maskt[:, pl.ds(2 * HALF, HALF)] = jnp.where(j < 64, 2.0, jnp.where((j < 64 + own // 2) & (col == 1), 3.0, NEG))

    def begin(h, at, kk, vv, mask):
        s = lax.dot_general(eq[h, pl.ds(at, HALF), :], kk, (((1,), (1,)), ((), ())),
                            preferred_element_type=F32)
        s = s * gain + mask
        m = jnp.broadcast_to(jnp.max(s, axis=1, keepdims=True), (HALF, width))
        w = jnp.exp2(s - across(m, s.shape[1])).astype(BF16)
        both = jnp.dot(w, with_ones(vv), preferred_element_type=F32)
        top[h, pl.ds(at, HALF), :] = m
        acc[h, pl.ds(at, HALF), :] = both[:, :width]
        total[h, pl.ds(at, HALF), :] = both[:, width:]

    def near(qd, first, count):
        def body(g, _):
            for part in range(2 * together):
                h, hf = g * together + part // 2, part % 2
                at = qd * QUAD + hf * HALF
                kk, vv = (jnp.concatenate([
                    e0[kv, h, pl.ds(at - BLOCK, 192), :],
                    e1[kv, h, pl.ds(at // 2 - BLOCK, BLOCK), :],
                    e2[kv, h, pl.ds((qd - 1) * BLOCK, BLOCK), :],
                    before[kv, h, pl.ds(3 * BLOCK, BLOCK)]], 0) for kv in range(2))
                begin(h, at, kk, vv, mask1[hf])
            return 0
        lax.fori_loop(first, first + count, body, 0)

    def nearest(first, count):
        def body(g, _):
            for n in range(together):
                h = g * together + n
                begin(h, 0, e0[0, h, pl.ds(0, HALF), :], e0[1, h, pl.ds(0, HALF), :], mask0[:, pl.ds(0, HALF)])
                kk, vv = (jnp.concatenate([
                    e0[kv, h, pl.ds(BLOCK, 192), :], e1[kv, h, pl.ds(0, BLOCK), :]], 0) for kv in range(2))
                begin(h, HALF, kk, vv, mask0[:, pl.ds(HALF, 2 * HALF)])
            return 0
        lax.fori_loop(first, first + count, body, 0)

    def merge(h, at, count, s, vv, lift):
        m = top[h, pl.ds(at, count), :]
        peak = jnp.max(s, axis=1, keepdims=True)
        if lift is not None:
            peak = peak * gain + lift
            s = s * gain
        fresh = jnp.maximum(m, peak)
        fade = jnp.exp2(m - fresh)
        w = jnp.exp2(s - across(fresh if lift is None else fresh - lift, s.shape[1])).astype(BF16)
        both = jnp.dot(w, with_ones(vv), preferred_element_type=F32)
        top[h, pl.ds(at, count), :] = fresh
        acc[h, pl.ds(at, count), :] = acc[h, pl.ds(at, count), :] * fade + both[:, :width]
        total[h, pl.ds(at, count), :] = total[h, pl.ds(at, count), :] * fade + both[:, width:]

    def scores(h, at, count, kk):
        return lax.dot_general(eq[h, pl.ds(at, count), :], kk, (((1,), (1,)), ((), ())),
                               preferred_element_type=F32)

    def extra():
        @pl.when(col == 1)
        def _():
            side_copy(0, me - 1).wait_recv()
            for kv in range(2):
                for h, part in enumerate(to_heads(far[kv, me - 1].astype(F32), tmp, heads)):
                    before[kv, h, pl.ds(3 * BLOCK, own)] = part

        @pl.when(col == 0)
        def _():
            for kv in range(2):
                for h in range(heads):
                    before[kv, h, pl.ds(3 * BLOCK, own)] = jnp.zeros((own, width), BF16)

    def previous():
        for kv in range(2):
            for part in range(2):
                tail_copy(kv, part).wait_recv()
            x = tail[kv, 0].astype(F32)
            two = halved(x)
            four = halved(two)
            y = tail[kv, 1].astype(F32)
            late = halved(y[:32])
            for h, part in enumerate(to_heads(x, tmp, heads)):
                before[kv, h, pl.ds(0, BLOCK), :] = part
            for h, part in enumerate(to_heads(two * 0.5, tmp, heads)):
                before[kv, h, pl.ds(96, 32), :] = part
            for h, part in enumerate(to_heads(four * 0.25, tmp, heads)):
                before[kv, h, pl.ds(176, 16), :] = part
            for h, part in enumerate(to_heads(late * 0.5, tmp, heads)):
                before[kv, h, pl.ds(160, 16), :] = part
            for h, part in enumerate(to_heads(y, tmp, heads)):
                before[kv, h, pl.ds(64, 32), :] = part[:32]
                before[kv, h, pl.ds(128, 32), :] = part[32:]

        def body(g, _):
            for n in range(together):
                h = g * together + n
                s = scores(h, 0, HALF, before[0, h]) * gain + maskt[:, pl.ds(0, 2 * HALF)]
                merge(h, 0, HALF, s, before[1, h], None)
                s = (scores(h, HALF, HALF, before[0, h, pl.ds(HALF, HALF), :]) * gain
                     + maskt[:, pl.ds(2 * HALF, HALF)])
                merge(h, HALF, HALF, s, before[1, h, pl.ds(HALF, HALF), :], None)
            return 0
        lax.fori_loop(0, groups, body, 0)

    def distant(r):
        odd = me - 2 * r + 1 - col
        even = me - 2 * r - col

        @pl.when(col == 1)
        def _():
            side_copy(0, even).wait_recv()

        @pl.when(col == 0)
        def _():
            side_copy(0, odd).wait_recv()
            side_copy(1, odd).wait_recv()

            @pl.when(jnp.logical_not(climbs))
            def _():
                side_copy(1, even).wait_recv()
        for kv in range(2):
            for n, b in enumerate((odd, even)):
                for h, part in enumerate(to_heads(far[kv, b].astype(F32), tmp, heads)):
                    fk[kv, h, pl.ds(n * own, own), :] = part
        place = lax.broadcasted_iota(jnp.int32, (1, 2 * own), 1)
        hide = jnp.where((col == 0) & (r == 1) & (place >= own // 2) & (place < own), NEG, 0.0)

        def body(g, _):
            for n in range(together * (rows // QUAD)):
                h, qd = g * together + n // (rows // QUAD), n % (rows // QUAD)
                at = qd * QUAD
                s = scores(h, at, QUAD, fk[0, h])
                if qd == 0:
                    s = s + hide
                merge(h, at, QUAD, s, fk[1, h], 3.0)
            return 0

        lax.fori_loop(0, heads // together, body, 0)

    def climb(kv, b):
        up_copy(kv, b).wait_recv()

        @pl.when(climbs)
        def _():
            up_copy(kv, b).start()

    def odd_turn(n):
        def at(turn, r):
            return (n == turn) & (r <= lev)

        @pl.when(n == 1)
        def _():
            climb(1, me - 1)

        for turn, r in ((1, 1), (4, 2), (6, 3)):
            @pl.when(at(turn, r))
            def _():
                climb(0, me - 2 * r)
                side_copy(0, me - 2 * r).start()

        for turn, r in ((2, 1), (5, 2), (6, 3)):
            @pl.when(at(turn, r))
            def _():
                climb(1, me - 2 * r)
                side_copy(1, me - 2 * r).start()

        for turn, r in ((3, 1), (5, 2), (7, 3)):
            @pl.when(at(turn, r))
            def _():
                climb(1, me - 2 * r - 1)
                if r == 1:
                    @pl.when(jnp.logical_not(climbs))
                    def _():
                        side_copy(1, me - 3).start()

        @pl.when((n >= 8) & (n - 4 <= lev))
        def _():
            b = me - 2 * (n - 4)
            for kv in range(2):
                climb(kv, b)
                side_copy(kv, b).start()
            climb(1, b - 1)

    def even_turn(n):
        def relay(kv, part):
            @pl.when(climbs)
            def _():
                thru_copy(kv, part).wait_recv()
                relay_copy(kv, part).start()

        def cross(r):
            @pl.when(r <= lev)
            def _():
                climb(0, me - 2 * r)
                side_copy(0, me - 2 * r).start()

        def rise(r):
            @pl.when((r <= lev) & climbs)
            def _():
                climb(1, me - 2 * r)

        @pl.when(n == 1)
        def _():
            cross(1)
            tail_copy(0, 0).start()
            tail_copy(0, 1).start()
            relay(0, 0)

        @pl.when(n == 2)
        def _():
            relay(0, 1)
            rise(1)

        @pl.when(n == 3)
        def _():
            cross(2)
            tail_copy(1, 0).start()
            tail_copy(1, 1).start()

        @pl.when(n == 4)
        def _():
            relay(1, 0)
            relay(1, 1)
            rise(2)

        @pl.when(n == 5)
        def _():
            cross(3)

        @pl.when(n == 7)
        def _():
            rise(3)

        @pl.when(n >= 8)
        def _():
            cross(n - 4)
            rise(n - 4)

    def turn(n, _):
        @pl.when(col == 1)
        def _():
            odd_turn(n)

        @pl.when(col == 0)
        def _():
            even_turn(n)

        first = jnp.where(lax.rem(n, 2) == 0, 0, early)
        count = jnp.where(lax.rem(n, 2) == 0, early, groups - early)

        @pl.when(n < 2)
        def _():
            nearest(first, count)

        @pl.when(n == 2)
        def _():
            extra()

        @pl.when((n == 2) | (n == 3))
        def _():
            for qd in range(1, rows // QUAD):
                near(qd, first, count)

        @pl.when((n == 6) & (me > 0))
        def _():
            previous()

        gone = jnp.where(n < 6, n - 3, n - 4)

        @pl.when((gone >= 1) & (gone <= lev) & (n != 6))
        def _():
            distant(gone)
        return 0

    lax.fori_loop(0, jnp.maximum(6, lev + 4) + 1, turn, 0)

    for c in range(rows // HALF):
        for h in range(heads):
            otmp[pl.ds(h, HALF, stride=heads), :] = (
                acc[h, pl.ds(c * HALF, HALF), :] / total[h, pl.ds(c * HALF, HALF), :])
        o_ref[pl.ds(c * HALF, HALF)] = otmp[...].reshape(HALF, heads, width).astype(BF16)

    @pl.when(col == 0)
    def _():
        side_copy(1, me).wait_send()
        side_copy(0, me).wait_send()
        for kv in range(2):
            for part in range(2):
                tail_copy(kv, part).wait_send()

        @pl.when(climbs)
        def _():
            up_copy(0, me).wait_send()
            for kv in range(2):
                for part in range(2):
                    relay_copy(kv, part).wait_send()

        @pl.when(lev < levels - 2)
        def _():
            up_copy(1, me).wait_send()

    @pl.when((col == 1) & climbs)
    def _():
        up_copy(0, me).wait_send()
        up_copy(1, me).wait_send()
        up_copy(1, me - 1).wait_send()
        for kv in range(2):
            for part in range(2):
                thru_copy(kv, part).wait_send()

    def sent(r, _):
        b = me - 2 * r
        side_copy(0, b).wait_send()

        @pl.when(climbs)
        def _():
            up_copy(0, b).wait_send()
            up_copy(1, b).wait_send()

        @pl.when(col == 1)
        def _():
            side_copy(1, b).wait_send()

            @pl.when(climbs)
            def _():
                up_copy(1, b - 1).wait_send()

            @pl.when((r == 1) & jnp.logical_not(climbs))
            def _():
                side_copy(1, b - 1).wait_send()
        return 0

    lax.fori_loop(1, lev + 1, sent, 0)


def shards(size, queries, keys, values):
    rows, heads, width = queries.shape
    own = rows // 8
    vmem = pl.BlockSpec(memory_space=pltpu.VMEM)
    return pl.pallas_call(
        functools.partial(kernel, size),
        out_shape=jax.ShapeDtypeStruct((rows, heads, width), BF16),
        in_specs=[vmem] * 3,
        out_specs=vmem,
        scratch_shapes=[
            pltpu.VMEM((2, size, own, heads, width), BF16),
            pltpu.VMEM((2, 2, BLOCK, heads, width), BF16),
            pltpu.VMEM((2, 2, BLOCK, heads, width), BF16),
            pltpu.VMEM((2, BLOCK, heads, width), BF16),
            pltpu.VMEM((heads, rows, width), BF16),
            pltpu.VMEM((2, heads, rows, width), BF16),
            pltpu.VMEM((2, heads, rows // 2 - BLOCK, width), BF16),
            pltpu.VMEM((2, heads, rows // 4 - BLOCK, width), BF16),
            pltpu.VMEM((2, heads, QUAD, width), BF16),
            pltpu.VMEM((2, heads, 2 * own, width), BF16),
            pltpu.VMEM((2, HALF, NEAR), F32),
            pltpu.VMEM((HALF, 3 * HALF), F32),
            pltpu.VMEM((HALF, 3 * HALF), F32),
            pltpu.VMEM((heads, rows, width), F32),
            pltpu.VMEM((heads, rows, width), F32),
            pltpu.VMEM((heads, rows, width), F32),
            pltpu.VMEM((80 * heads, width), F32),
            pltpu.VMEM((HALF * heads, width), F32),
            pltpu.SemaphoreType.DMA((2, size)),
            pltpu.SemaphoreType.DMA((2, size)),
            pltpu.SemaphoreType.DMA((2, size)),
            pltpu.SemaphoreType.DMA((2, 2)),
            pltpu.SemaphoreType.DMA((2, 2)),
            pltpu.SemaphoreType.DMA((2, 2)),
            pltpu.SemaphoreType.DMA((2, 2)),
        ],
        compiler_params=pltpu.CompilerParams(
            collective_id=0, has_side_effects=True, vmem_limit_bytes=60 * 2**20),
    )(queries, keys, values)


def solution(mesh):
    spec = P(("groups", "seq"), "heads", None)
    return jax.shard_map(
        functools.partial(shards, mesh.shape["seq"]),
        mesh=mesh, in_specs=(spec,) * 3, out_specs=spec, check_vma=False)
```

time: 66.3 us -> 40.4 us (0.61)
  Pallas kernels: 63.8 us -> 38 us
    pallas_call x1, Pallas kernels: 63.8 us -> 38 us  [shards(): pl.pallas_call(functools.partial(kernel, size), out_shape=jax.ShapeDtypeS...]
where the time goes in v2:
time: 40.4 us; the launch traced here: 40.2 us
  Pallas kernels  38 us (94%)
  local copies, waits for them, and re-layouts  2.26 us (6%)
    pallas_call x1, Pallas kernels, shards(): pl.pallas_call(functools.partial(kernel, size), out_shape=jax.ShapeDtypeS...  38 us
    unnamed x1, local copies, waits for them, and re-layouts  2.26 us

profile of v2, /device:TPU:28, one launch (start us, length us, event | category | flops | bytes accessed | tf_op | source)
XLA Modules:
  0.0 40.2 jit_solution(3437439476147742466)
XLA Ops:
  0.0 38.0 %shard_map.37 = bf16[512,8,128]{2,1,0:T(8,128)(2,1)} custom-call(bf16[512,8,128]{2,1,0:T(8,128)(2,1)} %q_ref.1, bf16[512,8,128]{2,1,0:T(8,128)(2,1)} %k_ref.1, bf16[512,8,128]{2,1,0:T(8,128)(2,1)} %v_ref.1), custom_call_target="tpu_custom_call" | custom-call | tf_op jit(solution)/shard_map/pallas_call | solution.py:512
  38.0 2.3 %copy.5 = bf16[512,8,128]{2,1,0:T(8,128)(2,1)} copy(bf16[512,8,128]{2,1,0:T(8,128)(2,1)} %shard_map.37) | data formatting | bytes 2097152

commit v3 on v2

--- a/solution.py
+++ b/solution.py
@@ -38,10 +38,10 @@
     return jnp.concatenate([values, jnp.ones_like(values)], 1)
 
 
-def kernel(size, q_ref, k_ref, v_ref, o_ref,
-           far, tail, thru, sendp, eq, e0, e1, e2, before, fk,
+def kernel(size, q_hbm, k_hbm, v_hbm, o_ref,
+           q_ref, k_ref, v_ref, far, tail, thru, sendp, eq, e0, e1, e2, before, fk,
            mask1, mask0, maskt, acc, top, total, tmp, otmp,
-           recv, up_send, side_send, t_send, t_recv, r_send, r_recv):
+           in_sem, recv, up_send, side_send, t_send, t_recv, r_send, r_recv):
     rows, heads, width = q_ref.shape
     own = rows // 8
     blocks = rows // BLOCK
@@ -89,6 +89,11 @@
                                 device_id_type=pl.DeviceIdType.MESH)
     pl.semaphore_signal(barrier, inc=1, device_id={"seq": pair}, device_id_type=pl.DeviceIdType.MESH)
 
+    loads = [pltpu.make_async_copy(src, dst, in_sem.at[n]) for n, (src, dst) in enumerate(
+        ((v_hbm, v_ref), (k_hbm, k_ref), (q_hbm, q_ref)))]
+    for load in loads:
+        load.start()
+
     def split(kv, c):
         x = sources[kv][pl.ds(c * BLOCK, BLOCK)].astype(F32)
         two = halved(x)
@@ -114,6 +119,7 @@
                     e2[kv, h, pl.ds(c * 16, 16), :] = part
 
     for kv in (1, 0):
+        loads[1 - kv].wait()
         for c in range(blocks):
             split(kv, c)
 
@@ -143,6 +149,7 @@
     for kv in range(2):
         for c in range(blocks):
             spread(kv, c)
+    loads[2].wait()
     for c in range(blocks):
         x = q_ref[pl.ds(c * BLOCK, BLOCK)].astype(F32)
         for h, part in enumerate(to_heads(x, tmp, heads)):
@@ -511,10 +518,13 @@
     vmem = pl.BlockSpec(memory_space=pltpu.VMEM)
     return pl.pallas_call(
         functools.partial(kernel, size),
-        out_shape=jax.ShapeDtypeStruct((rows, heads, width), BF16),
-        in_specs=[vmem] * 3,
+        out_shape=pltpu.VMEM((rows, heads, width), BF16),
+        in_specs=[pl.BlockSpec(memory_space=pl.ANY)] * 3,
         out_specs=vmem,
         scratch_shapes=[
+            pltpu.VMEM((rows, heads, width), BF16),
+            pltpu.VMEM((rows, heads, width), BF16),
+            pltpu.VMEM((rows, heads, width), BF16),
             pltpu.VMEM((2, size, own, heads, width), BF16),
             pltpu.VMEM((2, 2, BLOCK, heads, width), BF16),
             pltpu.VMEM((2, 2, BLOCK, heads, width), BF16),
@@ -533,6 +543,7 @@
             pltpu.VMEM((heads, rows, width), F32),
             pltpu.VMEM((80 * heads, width), F32),
             pltpu.VMEM((HALF * heads, width), F32),
+            pltpu.SemaphoreType.DMA((3,)),
             pltpu.SemaphoreType.DMA((2, size)),
             pltpu.SemaphoreType.DMA((2, size)),
             pltpu.SemaphoreType.DMA((2, size)),

time: 40.4 us -> 37 us (0.916)
  Pallas kernels: 38 us -> 35.8 us
  local copies, waits for them, and re-layouts: 2.26 us -> 0.97 us
    pallas_call x1, Pallas kernels: 38 us -> 35.8 us  [shards(): pl.pallas_call(functools.partial(kernel, size), out_shape=pltpu.VMEM((row...]
    unnamed x1, local copies, waits for them, and re-layouts: 2.26 us -> 0.97 us
where the time goes in v3:
time: 37 us; the launch traced here: 36.8 us
  Pallas kernels  35.8 us (97%)
  local copies, waits for them, and re-layouts  0.97 us (3%)
    pallas_call x1, Pallas kernels, shards(): pl.pallas_call(functools.partial(kernel, size), out_shape=pltpu.VMEM((row...  35.8 us
    unnamed x1, local copies, waits for them, and re-layouts  0.97 us

profile of v3, /device:TPU:28, one launch (start us, length us, event | category | flops | bytes accessed | tf_op | source)
XLA Modules:
  0.0 36.8 jit_solution(11997105783020847323)
XLA Ops:
  0.0 35.8 %shard_map.37 = bf16[512,8,128]{2,1,0:T(8,128)(2,1)S(1)} custom-call(bf16[512,8,128]{2,1,0:T(8,128)(2,1)} %q_hbm.1, bf16[512,8,128]{2,1,0:T(8,128)(2,1)} %k_hbm.1, bf16[512,8,128]{2,1,0:T(8,128)(2,1)} %v_hbm.1), custom_call_target="tpu_custom_call" | custom-call | tf_op jit(solution)/shard_map/pallas_call | solution.py:519
  35.8 1.0 %copy.5 = bf16[512,8,128]{2,1,0:T(8,128)(2,1)} copy(bf16[512,8,128]{2,1,0:T(8,128)(2,1)S(1)} %shard_map.37) | data formatting | bytes 2097152

commit v4 on v3

--- a/solution.py
+++ b/solution.py
@@ -53,6 +53,7 @@
     together = 2 - heads % 2
     groups = heads // together
     early = (groups + 1) // 2
+    share = heads // together
     climbs = lev < levels - 1
     pair = me + 1 - 2 * col
     up = jnp.minimum(me + 2, size - 1)
@@ -63,11 +64,17 @@
             src_ref=src, dst_ref=dst, send_sem=send, recv_sem=got,
             device_id={"seq": target}, device_id_type=pl.DeviceIdType.MESH)
 
-    def up_copy(kv, b):
-        return remote(far.at[kv, b], far.at[kv, b], up_send.at[kv, b], recv.at[kv, b], up)
-
-    def side_copy(kv, b):
-        return remote(far.at[kv, b], far.at[kv, b], side_send.at[kv, b], recv.at[kv, b], pair)
+    def up_copy(kv, b, hh):
+        place = far.at[kv, hh, b]
+        return remote(place, place, up_send.at[kv, hh, b], recv.at[kv, hh, b], up)
+
+    def side_copy(kv, b, hh):
+        place = far.at[kv, hh, b]
+        return remote(place, place, side_send.at[kv, hh, b], recv.at[kv, hh, b], pair)
+
+    def every(copy, kv, b, action):
+        for hh in range(together):
+            getattr(copy(kv, b, hh), action)()
 
     def tail_source(kv, part):
         return sources[kv].at[pl.ds(rows - BLOCK, BLOCK)] if part == 0 else sendp.at[kv]
@@ -99,7 +106,9 @@
         two = halved(x)
         four = halved(two)
         eight = halved(four)
-        far[kv, me, pl.ds(c * 8, 8)] = (eight * 0.125).astype(BF16)
+        eight = (eight * 0.125).astype(BF16)
+        for hh in range(together):
+            far[kv, hh, me, pl.ds(c * 8, 8)] = eight[:, hh * share:(hh + 1) * share]
         if c == blocks - 2:
             sendp[kv, pl.ds(0, 32)] = (two * 0.5).astype(BF16)
         if blocks - 4 <= c < blocks - 2:
@@ -127,21 +136,21 @@
 
     @pl.when(col == 0)
     def _():
-        side_copy(1, me).start()
-        side_copy(0, me).start()
+        every(side_copy, 1, me, "start")
+        every(side_copy, 0, me, "start")
 
         @pl.when(climbs)
         def _():
-            up_copy(0, me).start()
+            every(up_copy, 0, me, "start")
 
         @pl.when(lev < levels - 2)
         def _():
-            up_copy(1, me).start()
+            every(up_copy, 1, me, "start")
 
     @pl.when((col == 1) & climbs)
     def _():
-        up_copy(0, me).start()
-        up_copy(1, me).start()
+        every(up_copy, 0, me, "start")
+        every(up_copy, 1, me, "start")
         for kv in range(2):
             for part in range(2):
                 thru_copy(kv, part).start()
@@ -238,10 +247,11 @@
     def extra():
         @pl.when(col == 1)
         def _():
-            side_copy(0, me - 1).wait_recv()
+            every(side_copy, 0, me - 1, "wait_recv")
             for kv in range(2):
-                for h, part in enumerate(to_heads(far[kv, me - 1].astype(F32), tmp, heads)):
-                    before[kv, h, pl.ds(3 * BLOCK, own)] = part
+                for hh in range(together):
+                    for h, part in enumerate(to_heads(far[kv, hh, me - 1].astype(F32), tmp, share)):
+                        before[kv, hh * share + h, pl.ds(3 * BLOCK, own)] = part
 
         @pl.when(col == 0)
         def _():
@@ -281,47 +291,66 @@
             return 0
         lax.fori_loop(0, groups, body, 0)
 
-    def distant(r):
-        odd = me - 2 * r + 1 - col
-        even = me - 2 * r - col
-
-        @pl.when(col == 1)
-        def _():
-            side_copy(0, even).wait_recv()
-
-        @pl.when(col == 0)
-        def _():
-            side_copy(0, odd).wait_recv()
-            side_copy(1, odd).wait_recv()
-
-            @pl.when(jnp.logical_not(climbs))
-            def _():
-                side_copy(1, even).wait_recv()
-        for kv in range(2):
-            for n, b in enumerate((odd, even)):
-                for h, part in enumerate(to_heads(far[kv, b].astype(F32), tmp, heads)):
-                    fk[kv, h, pl.ds(n * own, own), :] = part
-        place = lax.broadcasted_iota(jnp.int32, (1, 2 * own), 1)
-        hide = jnp.where((col == 0) & (r == 1) & (place >= own // 2) & (place < own), NEG, 0.0)
+    def distant(lower):
+        upper = jnp.minimum(lower + 1, lev)
+        place = lax.broadcasted_iota(jnp.int32, (1, 4 * own), 1)
+        gone = (place >= 2 * own) & (upper == lower)
+        inner = (col == 0) & (lower == 1) & (place >= own // 2) & (place < own)
+        hides = [jnp.where(gone | inner, NEG, 0.0), jnp.where(gone, NEG, 0.0)]
+
+        def fetch(r, hh, spot):
+            odd = me - 2 * r + 1 - col
+            even = me - 2 * r - col
+
+            @pl.when((spot == 0) | (upper > lower))
+            def _():
+                @pl.when(col == 1)
+                def _():
+                    side_copy(0, even, hh).wait_recv()
+
+                    @pl.when(r == 3)
+                    def _():
+                        up_copy(1, even, hh).wait_recv()
+
+                        @pl.when(climbs)
+                        def _():
+                            up_copy(1, even, hh).start()
+
+                @pl.when(col == 0)
+                def _():
+                    side_copy(0, odd, hh).wait_recv()
+                    side_copy(1, odd, hh).wait_recv()
+
+                    @pl.when(jnp.logical_not(climbs))
+                    def _():
+                        side_copy(1, even, hh).wait_recv()
+            for kv in range(2):
+                for n, b in enumerate((odd, even)):
+                    for h, part in enumerate(to_heads(far[kv, hh, b].astype(F32), tmp, share)):
+                        fk[kv, hh * share + h, pl.ds((2 * spot + n) * own, own), :] = part
 
         def body(g, _):
             for n in range(together * (rows // QUAD)):
                 h, qd = g * together + n // (rows // QUAD), n % (rows // QUAD)
                 at = qd * QUAD
-                s = scores(h, at, QUAD, fk[0, h])
-                if qd == 0:
-                    s = s + hide
+                s = scores(h, at, QUAD, fk[0, h]) + hides[min(qd, 1)]
                 merge(h, at, QUAD, s, fk[1, h], 3.0)
             return 0
 
-        lax.fori_loop(0, heads // together, body, 0)
-
-    def climb(kv, b):
-        up_copy(kv, b).wait_recv()
-
-        @pl.when(climbs)
-        def _():
-            up_copy(kv, b).start()
+        for hh in range(together):
+            fetch(lower, hh, 0)
+            fetch(upper, hh, 1)
+            lax.fori_loop(hh * (groups // together), (hh + 1) * (groups // together), body, 0)
+
+    def climb(kv, b, side=None):
+        for hh in range(together):
+            up_copy(kv, b, hh).wait_recv()
+
+            @pl.when(climbs)
+            def _():
+                up_copy(kv, b, hh).start()
+            if side is not None:
+                side_copy(kv, b, hh).start()
 
     def odd_turn(n):
         def at(turn, r):
@@ -334,30 +363,27 @@
         for turn, r in ((1, 1), (4, 2), (6, 3)):
             @pl.when(at(turn, r))
             def _():
-                climb(0, me - 2 * r)
-                side_copy(0, me - 2 * r).start()
+                climb(0, me - 2 * r, True)
 
         for turn, r in ((2, 1), (5, 2), (6, 3)):
             @pl.when(at(turn, r))
             def _():
-                climb(1, me - 2 * r)
-                side_copy(1, me - 2 * r).start()
-
-        for turn, r in ((3, 1), (5, 2), (7, 3)):
+                climb(1, me - 2 * r, True)
+
+        for turn, r in ((3, 1), (5, 2)):
             @pl.when(at(turn, r))
             def _():
                 climb(1, me - 2 * r - 1)
                 if r == 1:
                     @pl.when(jnp.logical_not(climbs))
                     def _():
-                        side_copy(1, me - 3).start()
+                        every(side_copy, 1, me - 3, "start")
 
         @pl.when((n >= 8) & (n - 4 <= lev))
         def _():
             b = me - 2 * (n - 4)
             for kv in range(2):
-                climb(kv, b)
-                side_copy(kv, b).start()
+                climb(kv, b, True)
             climb(1, b - 1)
 
     def even_turn(n):
@@ -370,8 +396,7 @@
         def cross(r):
             @pl.when(r <= lev)
             def _():
-                climb(0, me - 2 * r)
-                side_copy(0, me - 2 * r).start()
+                climb(0, me - 2 * r, True)
 
         def rise(r):
             @pl.when((r <= lev) & climbs)
@@ -444,11 +469,12 @@
         def _():
             previous()
 
-        gone = jnp.where(n < 6, n - 3, n - 4)
-
-        @pl.when((gone >= 1) & (gone <= lev) & (n != 6))
-        def _():
-            distant(gone)
+        lower = jnp.where(n < 6, 1, ((n - 5) // 2) * 2 + 1)
+        ready = (n == 5) | (n >= 7) & ((lax.rem(n, 2) == 0) | (n - 4 == lev))
+
+        @pl.when(ready & (lower <= lev))
+        def _():
+            distant(lower)
         return 0
 
     lax.fori_loop(0, jnp.maximum(6, lev + 4) + 1, turn, 0)
@@ -461,52 +487,52 @@
 
     @pl.when(col == 0)
     def _():
-        side_copy(1, me).wait_send()
-        side_copy(0, me).wait_send()
+        every(side_copy, 1, me, "wait_send")
+        every(side_copy, 0, me, "wait_send")
         for kv in range(2):
             for part in range(2):
                 tail_copy(kv, part).wait_send()
 
         @pl.when(climbs)
         def _():
-            up_copy(0, me).wait_send()
+            every(up_copy, 0, me, "wait_send")
             for kv in range(2):
                 for part in range(2):
                     relay_copy(kv, part).wait_send()
 
         @pl.when(lev < levels - 2)
         def _():
-            up_copy(1, me).wait_send()
+            every(up_copy, 1, me, "wait_send")
 
     @pl.when((col == 1) & climbs)
     def _():
-        up_copy(0, me).wait_send()
-        up_copy(1, me).wait_send()
-        up_copy(1, me - 1).wait_send()
+        every(up_copy, 0, me, "wait_send")
+        every(up_copy, 1, me, "wait_send")
+        every(up_copy, 1, me - 1, "wait_send")
         for kv in range(2):
             for part in range(2):
                 thru_copy(kv, part).wait_send()
 
     def sent(r, _):
         b = me - 2 * r
-        side_copy(0, b).wait_send()
+        every(side_copy, 0, b, "wait_send")
 
         @pl.when(climbs)
         def _():
-            up_copy(0, b).wait_send()
-            up_copy(1, b).wait_send()
+            every(up_copy, 0, b, "wait_send")
+            every(up_copy, 1, b, "wait_send")
 
         @pl.when(col == 1)
         def _():
-            side_copy(1, b).wait_send()
+            every(side_copy, 1, b, "wait_send")
 
             @pl.when(climbs)
             def _():
-                up_copy(1, b - 1).wait_send()
+                every(up_copy, 1, b - 1, "wait_send")
 
             @pl.when((r == 1) & jnp.logical_not(climbs))
             def _():
-                side_copy(1, b - 1).wait_send()
+                every(side_copy, 1, b - 1, "wait_send")
         return 0
 
     lax.fori_loop(1, lev + 1, sent, 0)
@@ -515,6 +541,7 @@
 def shards(size, queries, keys, values):
     rows, heads, width = queries.shape
     own = rows // 8
+    parts = 2 - heads % 2
     vmem = pl.BlockSpec(memory_space=pltpu.VMEM)
     return pl.pallas_call(
         functools.partial(kernel, size),
@@ -525,7 +552,7 @@
             pltpu.VMEM((rows, heads, width), BF16),
             pltpu.VMEM((rows, heads, width), BF16),
             pltpu.VMEM((rows, heads, width), BF16),
-            pltpu.VMEM((2, size, own, heads, width), BF16),
+            pltpu.VMEM((2, parts, size, own, heads // parts, width), BF16),
             pltpu.VMEM((2, 2, BLOCK, heads, width), BF16),
             pltpu.VMEM((2, 2, BLOCK, heads, width), BF16),
             pltpu.VMEM((2, BLOCK, heads, width), BF16),
@@ -534,7 +561,7 @@
             pltpu.VMEM((2, heads, rows // 2 - BLOCK, width), BF16),
             pltpu.VMEM((2, heads, rows // 4 - BLOCK, width), BF16),
             pltpu.VMEM((2, heads, QUAD, width), BF16),
-            pltpu.VMEM((2, heads, 2 * own, width), BF16),
+            pltpu.VMEM((2, heads, 4 * own, width), BF16),
             pltpu.VMEM((2, HALF, NEAR), F32),
             pltpu.VMEM((HALF, 3 * HALF), F32),
             pltpu.VMEM((HALF, 3 * HALF), F32),
@@ -544,9 +571,9 @@
             pltpu.VMEM((80 * heads, width), F32),
             pltpu.VMEM((HALF * heads, width), F32),
             pltpu.SemaphoreType.DMA((3,)),
-            pltpu.SemaphoreType.DMA((2, size)),
-            pltpu.SemaphoreType.DMA((2, size)),
-            pltpu.SemaphoreType.DMA((2, size)),
+            pltpu.SemaphoreType.DMA((2, parts, size)),
+            pltpu.SemaphoreType.DMA((2, parts, size)),
+            pltpu.SemaphoreType.DMA((2, parts, size)),
             pltpu.SemaphoreType.DMA((2, 2)),
             pltpu.SemaphoreType.DMA((2, 2)),
             pltpu.SemaphoreType.DMA((2, 2)),

time: 37 us -> 35.6 us (0.962)
  Pallas kernels: 35.8 us -> 34.4 us
    pallas_call x1, Pallas kernels: 35.8 us -> 34.4 us  [shards(): pl.pallas_call(functools.partial(kernel, size), out_shape=pltpu.VMEM((row...]
where the time goes in v4:
time: 35.6 us; the launch traced here: 35.4 us
  Pallas kernels  34.4 us (97%)
  local copies, waits for them, and re-layouts  0.97 us (3%)
    pallas_call x1, Pallas kernels, shards(): pl.pallas_call(functools.partial(kernel, size), out_shape=pltpu.VMEM((row...  34.4 us
    unnamed x1, local copies, waits for them, and re-layouts  0.97 us

profile of v4, /device:TPU:28, one launch (start us, length us, event | category | flops | bytes accessed | tf_op | source)
XLA Modules:
  0.0 35.4 jit_solution(11735130505879825954)
XLA Ops:
  0.0 34.4 %shard_map.37 = bf16[512,8,128]{2,1,0:T(8,128)(2,1)S(1)} custom-call(bf16[512,8,128]{2,1,0:T(8,128)(2,1)} %q_hbm.1, bf16[512,8,128]{2,1,0:T(8,128)(2,1)} %k_hbm.1, bf16[512,8,128]{2,1,0:T(8,128)(2,1)} %v_hbm.1), custom_call_target="tpu_custom_call" | custom-call | tf_op jit(solution)/shard_map/pallas_call | solution.py:546
  34.5 1.0 %copy.5 = bf16[512,8,128]{2,1,0:T(8,128)(2,1)} copy(bf16[512,8,128]{2,1,0:T(8,128)(2,1)S(1)} %shard_map.37) | data formatting | bytes 2097152

commit v5 on v4

--- a/solution.py
+++ b/solution.py
@@ -143,9 +143,10 @@
         def _():
             every(up_copy, 0, me, "start")
 
-        @pl.when(lev < levels - 2)
-        def _():
-            every(up_copy, 1, me, "start")
+        for hh in range(together):
+            @pl.when(climbs if hh == 0 else lev < levels - 2)
+            def _():
+                up_copy(1, me, hh).start()
 
     @pl.when((col == 1) & climbs)
     def _():
@@ -181,14 +182,13 @@
     seen0 = jnp.where(j < 192, jnp.where((j <= i + BLOCK) & ((j >= BLOCK) | (i < BLOCK)), 1, 0),
                       jnp.where((j < 224) | (i >= BLOCK), 1, 0))
     mask0[:, pl.ds(HALF, 2 * HALF)] = jnp.where(seen0 > 0, jnp.where(j < 192, 0.0, 1.0), NEG)
-    last = jnp.where(j < 192 + own // 2, col, 0)
-    seent = jnp.where(j < 64, jnp.where(i < BLOCK, 1, 0),
-                      jnp.where(j < 128, jnp.where((j < 96) | (i >= BLOCK), 1, 0),
-                                jnp.where(j < 192, jnp.where(j < 160, 1, 0), last)))
+    ends = jnp.where(j < 192 + own // 2, col, 0)
     level = jnp.where(j < 64, 0.0, jnp.where(j < 128, 1.0, jnp.where(j < 192, 2.0, 3.0)))
-    maskt[:, pl.ds(0, 2 * HALF)] = jnp.where(seent > 0, level, NEG)
-    i, j = grid(HALF)
-    maskt[:, pl.ds(2 * HALF, HALF)] = jnp.where(j < 64, 2.0, jnp.where((j < 64 + own // 2) & (col == 1), 3.0, NEG))
+    for hf in range(2):
+        seent = jnp.where(j < 64, jnp.where(i < BLOCK, 1 - hf, 0),
+                          jnp.where(j < 128, jnp.where((j < 96) | (i >= BLOCK), 1 - hf, 0),
+                                    jnp.where(j < 192, jnp.where((j < 160) | (hf == 1), 1, 0), ends)))
+        maskt[pl.ds(hf * HALF, HALF), :] = jnp.where(seent > 0, level, NEG)
 
     def begin(h, at, kk, vv, mask):
         s = lax.dot_general(eq[h, pl.ds(at, HALF), :], kk, (((1,), (1,)), ((), ())),
@@ -283,16 +283,18 @@
         def body(g, _):
             for n in range(together):
                 h = g * together + n
-                s = scores(h, 0, HALF, before[0, h]) * gain + maskt[:, pl.ds(0, 2 * HALF)]
-                merge(h, 0, HALF, s, before[1, h], None)
-                s = (scores(h, HALF, HALF, before[0, h, pl.ds(HALF, HALF), :]) * gain
-                     + maskt[:, pl.ds(2 * HALF, HALF)])
-                merge(h, HALF, HALF, s, before[1, h, pl.ds(HALF, HALF), :], None)
+                s = scores(h, 0, QUAD, before[0, h]) * gain + maskt[...]
+                merge(h, 0, QUAD, s, before[1, h], None)
             return 0
         lax.fori_loop(0, groups, body, 0)
 
-    def distant(lower):
-        upper = jnp.minimum(lower + 1, lev)
+    def arrange(hh):
+        for h in range(hh * share, (hh + 1) * share):
+            for c in range(rows // HALF):
+                otmp[pl.ds(c * HALF * heads + h, HALF, stride=heads), :] = (
+                    acc[h, pl.ds(c * HALF, HALF), :] / total[h, pl.ds(c * HALF, HALF), :])
+
+    def distant(lower, upper, final):
         place = lax.broadcasted_iota(jnp.int32, (1, 4 * own), 1)
         gone = (place >= 2 * own) & (upper == lower)
         inner = (col == 0) & (lower == 1) & (place >= own // 2) & (place < own)
@@ -315,6 +317,11 @@
                         @pl.when(climbs)
                         def _():
                             up_copy(1, even, hh).start()
+
+                    if hh > 0:
+                        @pl.when((r == 2) & jnp.logical_not(climbs))
+                        def _():
+                            up_copy(1, even, hh).wait_recv()
 
                 @pl.when(col == 0)
                 def _():
@@ -342,8 +349,12 @@
             fetch(upper, hh, 1)
             lax.fori_loop(hh * (groups // together), (hh + 1) * (groups // together), body, 0)
 
-    def climb(kv, b, side=None):
-        for hh in range(together):
+            @pl.when(final)
+            def _():
+                arrange(hh)
+
+    def climb(kv, b, side=None, halves=tuple(range(together))):
+        for hh in halves:
             up_copy(kv, b, hh).wait_recv()
 
             @pl.when(climbs)
@@ -370,14 +381,41 @@
             def _():
                 climb(1, me - 2 * r, True)
 
-        for turn, r in ((3, 1), (5, 2)):
-            @pl.when(at(turn, r))
-            def _():
-                climb(1, me - 2 * r - 1)
-                if r == 1:
-                    @pl.when(jnp.logical_not(climbs))
-                    def _():
-                        every(side_copy, 1, me - 3, "start")
+        @pl.when(at(3, 1))
+        def _():
+            every(up_copy, 1, me - 3, "wait_recv")
+
+            @pl.when(lev == levels - 1)
+            def _():
+                for hh in range(1, together):
+                    side_copy(1, me - 3, hh).start()
+
+            @pl.when(climbs)
+            def _():
+                up_copy(1, me - 3, 0).start()
+
+            @pl.when(lev < levels - 2)
+            def _():
+                for hh in range(1, together):
+                    up_copy(1, me - 3, hh).start()
+
+        @pl.when(at(5, 2))
+        def _():
+            climb(1, me - 5, None, (0,))
+
+            @pl.when(lev == levels - 1)
+            def _():
+                side_copy(1, me - 5, 0).start()
+
+        @pl.when(at(5, 1) & (lev == levels - 2))
+        def _():
+            for hh in range(1, together):
+                up_copy(1, me - 3, hh).start()
+
+        @pl.when(at(5, 2) & climbs)
+        def _():
+            for hh in range(1, together):
+                climb(1, me - 5, None, (hh,))
 
         @pl.when((n >= 8) & (n - 4 <= lev))
         def _():
@@ -406,26 +444,45 @@
         @pl.when(n == 1)
         def _():
             cross(1)
-            tail_copy(0, 0).start()
-            tail_copy(0, 1).start()
+            for kv in range(2):
+                for part in range(2):
+                    tail_copy(kv, part).start()
             relay(0, 0)
 
         @pl.when(n == 2)
         def _():
             relay(0, 1)
-            rise(1)
+
+            @pl.when((lev >= 1) & climbs)
+            def _():
+                every(up_copy, 1, me - 2, "wait_recv")
+
+                @pl.when(lev < levels - 2)
+                def _():
+                    every(up_copy, 1, me - 2, "start")
 
         @pl.when(n == 3)
         def _():
             cross(2)
-            tail_copy(1, 0).start()
-            tail_copy(1, 1).start()
 
         @pl.when(n == 4)
         def _():
             relay(1, 0)
             relay(1, 1)
-            rise(2)
+
+            @pl.when((lev >= 2) & climbs)
+            def _():
+                climb(1, me - 4, None, (0,))
+
+            @pl.when((lev >= 1) & (lev == levels - 2))
+            def _():
+                for hh in range(1, together):
+                    up_copy(1, me - 2, hh).start()
+
+            @pl.when((lev >= 2) & climbs)
+            def _():
+                for hh in range(1, together):
+                    climb(1, me - 4, None, (hh,))
 
         @pl.when(n == 5)
         def _():
@@ -469,21 +526,25 @@
         def _():
             previous()
 
-        lower = jnp.where(n < 6, 1, ((n - 5) // 2) * 2 + 1)
-        ready = (n == 5) | (n >= 7) & ((lax.rem(n, 2) == 0) | (n - 4 == lev))
-
-        @pl.when(ready & (lower <= lev))
-        def _():
-            distant(lower)
+        upper = jnp.where(n < 6, n - 3, n - 4)
+        lower = jnp.maximum(upper - 1, 1)
+        even = lax.rem(lev - upper, 2) == 0
+
+        @pl.when((n >= 4) & (n != 6) & (upper <= lev) & even)
+        def _():
+            distant(lower, upper, (n >= 7) & (upper == lev))
         return 0
 
     lax.fori_loop(0, jnp.maximum(6, lev + 4) + 1, turn, 0)
 
+    @pl.when(lev < 3)
+    def _():
+        for hh in range(together):
+            arrange(hh)
+
     for c in range(rows // HALF):
-        for h in range(heads):
-            otmp[pl.ds(h, HALF, stride=heads), :] = (
-                acc[h, pl.ds(c * HALF, HALF), :] / total[h, pl.ds(c * HALF, HALF), :])
-        o_ref[pl.ds(c * HALF, HALF)] = otmp[...].reshape(HALF, heads, width).astype(BF16)
+        o_ref[pl.ds(c * HALF, HALF)] = (
+            otmp[pl.ds(c * HALF * heads, HALF * heads), :].reshape(HALF, heads, width).astype(BF16))
 
     @pl.when(col == 0)
     def _():
@@ -500,9 +561,10 @@
                 for part in range(2):
                     relay_copy(kv, part).wait_send()
 
-        @pl.when(lev < levels - 2)
-        def _():
-            every(up_copy, 1, me, "wait_send")
+        for hh in range(together):
+            @pl.when(climbs if hh == 0 else lev < levels - 2)
+            def _():
+                up_copy(1, me, hh).wait_send()
 
     @pl.when((col == 1) & climbs)
     def _():
@@ -520,7 +582,11 @@
         @pl.when(climbs)
         def _():
             every(up_copy, 0, b, "wait_send")
-            every(up_copy, 1, b, "wait_send")
+
+            for hh in range(together):
+                @pl.when((hh > 0) | (col == 1) | (r > 1) | (lev < levels - 2))
+                def _():
+                    up_copy(1, b, hh).wait_send()
 
         @pl.when(col == 1)
         def _():
@@ -530,9 +596,10 @@
             def _():
                 every(up_copy, 1, b - 1, "wait_send")
 
-            @pl.when((r == 1) & jnp.logical_not(climbs))
-            def _():
-                every(side_copy, 1, b - 1, "wait_send")
+            for hh in range(together):
+                @pl.when((r == (2 if hh == 0 else 1)) & jnp.logical_not(climbs))
+                def _():
+                    side_copy(1, b - 1, hh).wait_send()
         return 0
 
     lax.fori_loop(1, lev + 1, sent, 0)
@@ -564,12 +631,12 @@
             pltpu.VMEM((2, heads, 4 * own, width), BF16),
             pltpu.VMEM((2, HALF, NEAR), F32),
             pltpu.VMEM((HALF, 3 * HALF), F32),
-            pltpu.VMEM((HALF, 3 * HALF), F32),
+            pltpu.VMEM((QUAD, QUAD), F32),
             pltpu.VMEM((heads, rows, width), F32),
             pltpu.VMEM((heads, rows, width), F32),
             pltpu.VMEM((heads, rows, width), F32),
             pltpu.VMEM((80 * heads, width), F32),
-            pltpu.VMEM((HALF * heads, width), F32),
+            pltpu.VMEM((rows * heads, width), F32),
             pltpu.SemaphoreType.DMA((3,)),
             pltpu.SemaphoreType.DMA((2, parts, size)),
             pltpu.SemaphoreType.DMA((2, parts, size)),

time: 35.6 us -> 34.2 us (0.961)
  Pallas kernels: 34.4 us -> 33.1 us
    pallas_call x1, Pallas kernels: 34.4 us -> 33.1 us  [shards(): pl.pallas_call(functools.partial(kernel, size), out_shape=pltpu.VMEM((row...]
where the time goes in v5:
time: 34.2 us; the launch traced here: 34.1 us
  Pallas kernels  33.1 us (97%)
  local copies, waits for them, and re-layouts  0.97 us (3%)
    pallas_call x1, Pallas kernels, shards(): pl.pallas_call(functools.partial(kernel, size), out_shape=pltpu.VMEM((row...  33.1 us
    unnamed x1, local copies, waits for them, and re-layouts  0.97 us

profile of v5, /device:TPU:28, one launch (start us, length us, event | category | flops | bytes accessed | tf_op | source)
XLA Modules:
  0.0 34.1 jit_solution(3206209407642664975)
XLA Ops:
  0.0 33.1 %shard_map.37 = bf16[512,8,128]{2,1,0:T(8,128)(2,1)S(1)} custom-call(bf16[512,8,128]{2,1,0:T(8,128)(2,1)} %q_hbm.1, bf16[512,8,128]{2,1,0:T(8,128)(2,1)} %k_hbm.1, bf16[512,8,128]{2,1,0:T(8,128)(2,1)} %v_hbm.1), custom_call_target="tpu_custom_call" | custom-call | tf_op jit(solution)/shard_map/pallas_call | solution.py:613
  33.1 1.0 %copy.5 = bf16[512,8,128]{2,1,0:T(8,128)(2,1)} copy(bf16[512,8,128]{2,1,0:T(8,128)(2,1)S(1)} %shard_map.37) | data formatting | bytes 2097152

commit v6 on v5

--- a/solution.py
+++ b/solution.py
@@ -281,12 +281,12 @@
                 before[kv, h, pl.ds(128, 32), :] = part[32:]
 
         def body(g, _):
-            for n in range(together):
-                h = g * together + n
+            for n in range(share):
+                h = g * share + n
                 s = scores(h, 0, QUAD, before[0, h]) * gain + maskt[...]
                 merge(h, 0, QUAD, s, before[1, h], None)
             return 0
-        lax.fori_loop(0, groups, body, 0)
+        lax.fori_loop(0, together, body, 0)
 
     def arrange(hh):
         for h in range(hh * share, (hh + 1) * share):
@@ -337,8 +337,8 @@
                         fk[kv, hh * share + h, pl.ds((2 * spot + n) * own, own), :] = part
 
         def body(g, _):
-            for n in range(together * (rows // QUAD)):
-                h, qd = g * together + n // (rows // QUAD), n % (rows // QUAD)
+            for n in range(share * (rows // QUAD)):
+                h, qd = g * share + n // (rows // QUAD), n % (rows // QUAD)
                 at = qd * QUAD
                 s = scores(h, at, QUAD, fk[0, h]) + hides[min(qd, 1)]
                 merge(h, at, QUAD, s, fk[1, h], 3.0)
@@ -347,7 +347,7 @@
         for hh in range(together):
             fetch(lower, hh, 0)
             fetch(upper, hh, 1)
-            lax.fori_loop(hh * (groups // together), (hh + 1) * (groups // together), body, 0)
+            lax.fori_loop(hh, hh + 1, body, 0)
 
             @pl.when(final)
             def _():
@@ -522,7 +522,7 @@
             for qd in range(1, rows // QUAD):
                 near(qd, first, count)
 
-        @pl.when((n == 6) & (me > 0))
+        @pl.when((n == jnp.where(lev == 2, 5, 6)) & (me > 0))
         def _():
             previous()
 

time: 34.2 us -> 33.3 us (0.974)
  Pallas kernels: 33.1 us -> 32.1 us
    pallas_call x1, Pallas kernels: 33.1 us -> 32.1 us  [shards(): pl.pallas_call(functools.partial(kernel, size), out_shape=pltpu.VMEM((row...]
where the time goes in v6:
time: 33.3 us; the launch traced here: 33.1 us
  Pallas kernels  32.1 us (96%)
  local copies, waits for them, and re-layouts  0.97 us (3%)
    pallas_call x1, Pallas kernels, shards(): pl.pallas_call(functools.partial(kernel, size), out_shape=pltpu.VMEM((row...  32.1 us
    unnamed x1, local copies, waits for them, and re-layouts  0.97 us

profile of v6, /device:TPU:28, one launch (start us, length us, event | category | flops | bytes accessed | tf_op | source)
XLA Modules:
  0.0 33.1 jit_solution(4892113321265722381)
XLA Ops:
  0.0 32.1 %shard_map.37 = bf16[512,8,128]{2,1,0:T(8,128)(2,1)S(1)} custom-call(bf16[512,8,128]{2,1,0:T(8,128)(2,1)} %q_hbm.1, bf16[512,8,128]{2,1,0:T(8,128)(2,1)} %k_hbm.1, bf16[512,8,128]{2,1,0:T(8,128)(2,1)} %v_hbm.1), custom_call_target="tpu_custom_call" | custom-call | tf_op jit(solution)/shard_map/pallas_call | solution.py:613
  32.1 1.0 %copy.5 = bf16[512,8,128]{2,1,0:T(8,128)(2,1)} copy(bf16[512,8,128]{2,1,0:T(8,128)(2,1)S(1)} %shard_map.37) | data formatting | bytes 2097152

commit v7 on v6

--- a/solution.py
+++ b/solution.py
@@ -203,8 +203,8 @@
 
     def near(qd, first, count):
         def body(g, _):
-            for part in range(2 * together):
-                h, hf = g * together + part // 2, part % 2
+            for part in range(2 * share):
+                h, hf = g * share + part // 2, part % 2
                 at = qd * QUAD + hf * HALF
                 kk, vv = (jnp.concatenate([
                     e0[kv, h, pl.ds(at - BLOCK, 192), :],
@@ -217,8 +217,8 @@
 
     def nearest(first, count):
         def body(g, _):
-            for n in range(together):
-                h = g * together + n
+            for n in range(share):
+                h = g * share + n
                 begin(h, 0, e0[0, h, pl.ds(0, HALF), :], e0[1, h, pl.ds(0, HALF), :], mask0[:, pl.ds(0, HALF)])
                 kk, vv = (jnp.concatenate([
                     e0[kv, h, pl.ds(BLOCK, 192), :], e1[kv, h, pl.ds(0, BLOCK), :]], 0) for kv in range(2))
@@ -506,8 +506,8 @@
         def _():
             even_turn(n)
 
-        first = jnp.where(lax.rem(n, 2) == 0, 0, early)
-        count = jnp.where(lax.rem(n, 2) == 0, early, groups - early)
+        first = lax.rem(n, 2)
+        count = jnp.where(first < together, 1, 0)
 
         @pl.when(n < 2)
         def _():

time: 33.3 us -> 33.3 us (level)
  no operation moved by 1% of the time
where the time goes in v7:
time: 33.3 us; the launch traced here: 33.1 us
  Pallas kernels  32.1 us (96%)
  local copies, waits for them, and re-layouts  0.97 us (3%)
    pallas_call x1, Pallas kernels, shards(): pl.pallas_call(functools.partial(kernel, size), out_shape=pltpu.VMEM((row...  32.1 us
    unnamed x1, local copies, waits for them, and re-layouts  0.97 us

profile of v7, /device:TPU:28, one launch (start us, length us, event | category | flops | bytes accessed | tf_op | source)
XLA Modules:
  0.0 33.1 jit_solution(792479692737449742)
XLA Ops:
  0.0 32.1 %shard_map.37 = bf16[512,8,128]{2,1,0:T(8,128)(2,1)S(1)} custom-call(bf16[512,8,128]{2,1,0:T(8,128)(2,1)} %q_hbm.1, bf16[512,8,128]{2,1,0:T(8,128)(2,1)} %k_hbm.1, bf16[512,8,128]{2,1,0:T(8,128)(2,1)} %v_hbm.1), custom_call_target="tpu_custom_call" | custom-call | tf_op jit(solution)/shard_map/pallas_call | solution.py:613
  32.2 1.0 %copy.5 = bf16[512,8,128]{2,1,0:T(8,128)(2,1)} copy(bf16[512,8,128]{2,1,0:T(8,128)(2,1)S(1)} %shard_map.37) | data formatting | bytes 2097152
